TPU v7x, 256 devices: a whole 4x4x8 slice. The times are simulated.
256 devices in a mesh: bulk: 16 (over x, y), grp: 16 (over z, core).
Axes of the slice: x: 4, y: 4, z: 8, core: 2. Of those that a mesh axis runs over, the one named last changes fastest.
Arguments:
- embeddings: bfloat16 [131072, 768], P(('bulk', 'grp')), may hold values from -6 to 6
- cluster_ids: int32 [131072, 1], P(('bulk', 'grp')), may hold values from 0 to 15; in each aligned block of 512 rows (0 to 511, 512 to 1023, ...) at most 48 rows name the same one
- row_order: int32 [131072], P(('bulk', 'grp')), may hold values from 0 to 131071, each once
Outputs:
- earlier_max: float32 [131072], P(('bulk', 'grp'))
Inputs may be any that keep to these rules, and one draw needn't show every extreme that they name: `cluster_ids`: the rows of one device name any one cluster at most 48 times; some cluster is named exactly 48 times by some device's rows.
All inputs are finite; a program needn't handle non-finite values.
Results may differ from a plain program's by a relative error of at most 0.0013.
Values may be sent and summed in bfloat16 or wider, within the bound.
A program may use at most 64 MiB of HBM per device.

v0:
```python
import jax
import jax.numpy as jnp
from jax import lax
from jax.sharding import PartitionSpec as P


def on_device(embeddings, cluster_ids, row_order):
    rows = embeddings.shape[0]
    width = embeddings.shape[1]
    owners = lax.axis_size("bulk")
    capacity = 3 * rows // (2 * owners)
    values = embeddings.astype(jnp.float32)
    unit = (values * lax.rsqrt(jnp.sum(values * values, axis=1, keepdims=True) + 1e-06)).astype(
        jnp.bfloat16
    )
    target = cluster_ids[:, 0]
    onehot = (target[:, None] == jnp.arange(owners, dtype=jnp.int32)[None, :]).astype(jnp.int32)
    before = jnp.cumsum(onehot, axis=0) - onehot
    rank = jnp.sum(before * onehot, axis=1)
    slot = target * capacity + rank
    send_rows = jnp.zeros((owners * capacity, width), jnp.bfloat16).at[slot].set(unit)
    send_order = jnp.full((owners * capacity,), -1, jnp.int32).at[slot].set(row_order)
    recv_rows, recv_order = (
        lax.all_to_all(send_rows, "bulk", split_axis=0, concat_axis=0, tiled=True),
        lax.all_to_all(send_order, "bulk", split_axis=0, concat_axis=0, tiled=True),
    )
    initial = jnp.full((recv_rows.shape[0],), -1.0, jnp.float32)

    def fold_piece(best, piece):
        key_rows, key_order = piece
        scores = lax.dot_general(
            recv_rows, key_rows, (((1,), (1,)), ((), ())), preferred_element_type=jnp.float32
        )
        usable = (key_order[None, :] >= 0) & (key_order[None, :] < recv_order[:, None])
        return jnp.maximum(best, jnp.max(jnp.where(usable, scores, jnp.float32(-1.0)), axis=1))

    all_rows, all_order = (
        lax.all_gather(recv_rows, "grp", axis=0, tiled=True),
        lax.all_gather(recv_order, "grp", axis=0, tiled=True),
    )
    block = recv_rows.shape[0]
    pieces = all_rows.shape[0] // block

    def step_block(index, best):
        begin = index * block
        piece_rows = lax.dynamic_slice_in_dim(all_rows, begin, block, 0)
        piece_order = lax.dynamic_slice_in_dim(all_order, begin, block, 0)
        return fold_piece(best, (piece_rows, piece_order))

    best = lax.fori_loop(0, pieces, step_block, initial)
    returned = lax.all_to_all(best, "bulk", split_axis=0, concat_axis=0, tiled=True)
    return returned[slot]


def solution(mesh):
    return jax.shard_map(
        on_device,
        mesh=mesh,
        in_specs=(P(("bulk", "grp"), None), P(("bulk", "grp"), None), P(("bulk", "grp"))),
        out_specs=P(("bulk", "grp")),
        check_vma=False,
    )
```

profile of v0, /device:TPU:8, one launch (start us, length us, event | category | flops | bytes accessed | tf_op | source)
XLA Modules:
  0.0 218.4 jit_solution(13672971153205996998)
XLA Ops:
  6.5 0.7 fusion.12
  7.2 1.1 reduce-window.6
  8.6 0.8 fusion.11
  9.4 0.7 compare_select_fusion
  10.1 1.4 fusion.3
  11.5 3.5 %scatter_custom_fusion.1 = bf16[768,768]{1,0:T(8,128)(2,1)S(1)} fusion(s32[512]{0:T(512)S(1)} %bitcast.47, bf16[512,768]{1,0:T(8,128)(2,1)} %param.5, f32[512]{0:T(512)S(1)} %add_rsqrt_fusion, bf16[]{:T(256)} %constant.56.clone.1), kind=kCustom, calls=%fused_computation.13 | custom fusion | flops 1179648 | bytes 1968130 | tf_op jit(solution)/shard_map/scatter | solution.py:21
  15.0 24.3 %all_to_all.36 = bf16[16,48,768]{2,1,0:T(8,128)(2,1)} all-to-all(bf16[16,48,768]{2,1,0:T(8,128)(2,1)S(1)} %bitcast.40), channel_id=1, replica_groups=mesh['bulk'=16,'grp'=16] {'bulk'}, dimensions={0} | all-to-all | bytes 2359296 | tf_op jit(solution)/shard_map/all_to_all | solution.py:24
  39.3 2.6 %scatter_custom_fusion = s32[768]{0:T(1024)S(1)} fusion(s32[512]{0:T(512)S(1)} %bitcast.48, s32[512]{0:T(512)} %param.7, s32[]{:T(128)} %constant.61.clone.1), kind=kCustom, calls=%fused_computation.28 | custom fusion | bytes 3584 | tf_op jit(solution)/shard_map/scatter | solution.py:22
  42.6 5.1 %all-to-all-start = ((s32[16,48,1]{1,2,0:T(1,128)}), s32[16,48,1]{1,2,0:T(1,128)S(1)}, u32[]{:S(2)}, u32[]{:S(2)}) async-start(s32[16,48,1]{1,2,0:T(1,128)} %bitcast.5), calls=%async_computation | async-start | bytes 16384 | tf_op jit(solution)/shard_map/all_to_all | solution.py:25
  47.7 6.2 %all-to-all-done = s32[16,48,1]{1,2,0:T(1,128)S(1)} async-done(((s32[16,48,1]{1,2,0:T(1,128)}), s32[16,48,1]{1,2,0:T(1,128)S(1)}, u32[]{:S(2)}, u32[]{:S(2)}) %all-to-all-start) | async-done | bytes 3104 | tf_op jit(solution)/shard_map/all_to_all | solution.py:25
  55.3 20.8 %all-gather = s32[16,1,768]{2,1,0:T(1,128)S(1)} all-gather(s32[1,1,768]{2,1,0:T(1,128)S(1)} %reshape.58), channel_id=1, replica_groups=mesh['bulk'=16,'grp'=16] {'grp'}, dimensions={0}, use_global_device_ids=true | all-gather | bytes 52224 | tf_op jit(solution)/shard_map/all_gather | solution.py:39
  76.1 69.4 %all-gather.3.cloned.1.call-done = bf16[12288,768]{1,0:T(8,128)(2,1)} async-done(((bf16[768,768]{1,0:T(8,128)(2,1)}), bf16[12288,768]{1,0:T(8,128)(2,1)}) %all-gather.3.cloned.1.call-update) | async-done | bytes 18874384 | tf_op jit(solution)/shard_map/all_gather | solution.py:38
  145.5 47.2 %while.14 = (s32[]{:T(128)}, f32[768]{0:T(1024)S(1)}, s32[12288]{0:T(1024)S(1)}, s32[768]{0:T(1024)S(1)}, bf16[12288,768]{1,0:T(8,128)(2,1)}, /*index=5*/bf16[76...) while((s32[]{:T(128)}, f32[768]{0:T(1024)S(1)}, s32[12288]{0:T(1024)S(1)}, ...), condition=%wide.region_8.9_spmd.clone, body=%wide.region_6.8_spmd.clone.sunk | while | flops 908330496 | bytes 2385573 | solution.py:50
  145.6 2.8 %fusion.21 = f32[768]{0:T(1024)S(1)} fusion(bf16[768,768]{1,0:T(8,128)(2,1)} %get-tuple-element.216, bf16[12288,768]{1,0:T(8,128)(2,1)} %get-tuple-element.215, s32[]{:T(128)S(6)} %select_n.32, s32[768]{0:T(1024)S(1)} %get-tuple-element.214, s32[768]{0:T(1024)S(1)} %get-tuple-element.189, pred[768]{0:T(1024)(128)(4,1)S(1)} %get-tuple-element.190), kind=kOutput, calls=%fused_computation.4.clone.1 | convolution fusion | flops 908328192 | bytes 2369284 | tf_op jit(solution)/shard_map/while/body/eval_jaxpr/dot_general | solution.py:31
  148.6 2.8 %fusion.21 = f32[768]{0:T(1024)S(1)} fusion(bf16[768,768]{1,0:T(8,128)(2,1)} %get-tuple-element.216, bf16[12288,768]{1,0:T(8,128)(2,1)} %get-tuple-element.215, s32[]{:T(128)S(6)} %select_n.32, s32[768]{0:T(1024)S(1)} %get-tuple-element.214, s32[768]{0:T(1024)S(1)} %get-tuple-element.189, pred[768]{0:T(1024)(128)(4,1)S(1)} %get-tuple-element.190), kind=kOutput, calls=%fused_computation.4.clone.1 | convolution fusion | flops 908328192 | bytes 2369284 | tf_op jit(solution)/shard_map/while/body/eval_jaxpr/dot_general | solution.py:31
  151.5 2.8 %fusion.21 = f32[768]{0:T(1024)S(1)} fusion(bf16[768,768]{1,0:T(8,128)(2,1)} %get-tuple-element.216, bf16[12288,768]{1,0:T(8,128)(2,1)} %get-tuple-element.215, s32[]{:T(128)S(6)} %select_n.32, s32[768]{0:T(1024)S(1)} %get-tuple-element.214, s32[768]{0:T(1024)S(1)} %get-tuple-element.189, pred[768]{0:T(1024)(128)(4,1)S(1)} %get-tuple-element.190), kind=kOutput, calls=%fused_computation.4.clone.1 | convolution fusion | flops 908328192 | bytes 2369284 | tf_op jit(solution)/shard_map/while/body/eval_jaxpr/dot_general | solution.py:31
  154.5 2.8 %fusion.21 = f32[768]{0:T(1024)S(1)} fusion(bf16[768,768]{1,0:T(8,128)(2,1)} %get-tuple-element.216, bf16[12288,768]{1,0:T(8,128)(2,1)} %get-tuple-element.215, s32[]{:T(128)S(6)} %select_n.32, s32[768]{0:T(1024)S(1)} %get-tuple-element.214, s32[768]{0:T(1024)S(1)} %get-tuple-element.189, pred[768]{0:T(1024)(128)(4,1)S(1)} %get-tuple-element.190), kind=kOutput, calls=%fused_computation.4.clone.1 | convolution fusion | flops 908328192 | bytes 2369284 | tf_op jit(solution)/shard_map/while/body/eval_jaxpr/dot_general | solution.py:31
  157.4 2.8 %fusion.21 = f32[768]{0:T(1024)S(1)} fusion(bf16[768,768]{1,0:T(8,128)(2,1)} %get-tuple-element.216, bf16[12288,768]{1,0:T(8,128)(2,1)} %get-tuple-element.215, s32[]{:T(128)S(6)} %select_n.32, s32[768]{0:T(1024)S(1)} %get-tuple-element.214, s32[768]{0:T(1024)S(1)} %get-tuple-element.189, pred[768]{0:T(1024)(128)(4,1)S(1)} %get-tuple-element.190), kind=kOutput, calls=%fused_computation.4.clone.1 | convolution fusion | flops 908328192 | bytes 2369284 | tf_op jit(solution)/shard_map/while/body/eval_jaxpr/dot_general | solution.py:31
  160.4 2.8 %fusion.21 = f32[768]{0:T(1024)S(1)} fusion(bf16[768,768]{1,0:T(8,128)(2,1)} %get-tuple-element.216, bf16[12288,768]{1,0:T(8,128)(2,1)} %get-tuple-element.215, s32[]{:T(128)S(6)} %select_n.32, s32[768]{0:T(1024)S(1)} %get-tuple-element.214, s32[768]{0:T(1024)S(1)} %get-tuple-element.189, pred[768]{0:T(1024)(128)(4,1)S(1)} %get-tuple-element.190), kind=kOutput, calls=%fused_computation.4.clone.1 | convolution fusion | flops 908328192 | bytes 2369284 | tf_op jit(solution)/shard_map/while/body/eval_jaxpr/dot_general | solution.py:31
  163.3 2.8 %fusion.21 = f32[768]{0:T(1024)S(1)} fusion(bf16[768,768]{1,0:T(8,128)(2,1)} %get-tuple-element.216, bf16[12288,768]{1,0:T(8,128)(2,1)} %get-tuple-element.215, s32[]{:T(128)S(6)} %select_n.32, s32[768]{0:T(1024)S(1)} %get-tuple-element.214, s32[768]{0:T(1024)S(1)} %get-tuple-element.189, pred[768]{0:T(1024)(128)(4,1)S(1)} %get-tuple-element.190), kind=kOutput, calls=%fused_computation.4.clone.1 | convolution fusion | flops 908328192 | bytes 2369284 | tf_op jit(solution)/shard_map/while/body/eval_jaxpr/dot_general | solution.py:31
  166.3 2.8 %fusion.21 = f32[768]{0:T(1024)S(1)} fusion(bf16[768,768]{1,0:T(8,128)(2,1)} %get-tuple-element.216, bf16[12288,768]{1,0:T(8,128)(2,1)} %get-tuple-element.215, s32[]{:T(128)S(6)} %select_n.32, s32[768]{0:T(1024)S(1)} %get-tuple-element.214, s32[768]{0:T(1024)S(1)} %get-tuple-element.189, pred[768]{0:T(1024)(128)(4,1)S(1)} %get-tuple-element.190), kind=kOutput, calls=%fused_computation.4.clone.1 | convolution fusion | flops 908328192 | bytes 2369284 | tf_op jit(solution)/shard_map/while/body/eval_jaxpr/dot_general | solution.py:31
  169.2 2.8 %fusion.21 = f32[768]{0:T(1024)S(1)} fusion(bf16[768,768]{1,0:T(8,128)(2,1)} %get-tuple-element.216, bf16[12288,768]{1,0:T(8,128)(2,1)} %get-tuple-element.215, s32[]{:T(128)S(6)} %select_n.32, s32[768]{0:T(1024)S(1)} %get-tuple-element.214, s32[768]{0:T(1024)S(1)} %get-tuple-element.189, pred[768]{0:T(1024)(128)(4,1)S(1)} %get-tuple-element.190), kind=kOutput, calls=%fused_computation.4.clone.1 | convolution fusion | flops 908328192 | bytes 2369284 | tf_op jit(solution)/shard_map/while/body/eval_jaxpr/dot_general | solution.py:31
  172.2 2.8 %fusion.21 = f32[768]{0:T(1024)S(1)} fusion(bf16[768,768]{1,0:T(8,128)(2,1)} %get-tuple-element.216, bf16[12288,768]{1,0:T(8,128)(2,1)} %get-tuple-element.215, s32[]{:T(128)S(6)} %select_n.32, s32[768]{0:T(1024)S(1)} %get-tuple-element.214, s32[768]{0:T(1024)S(1)} %get-tuple-element.189, pred[768]{0:T(1024)(128)(4,1)S(1)} %get-tuple-element.190), kind=kOutput, calls=%fused_computation.4.clone.1 | convolution fusion | flops 908328192 | bytes 2369284 | tf_op jit(solution)/shard_map/while/body/eval_jaxpr/dot_general | solution.py:31
  175.1 2.8 %fusion.21 = f32[768]{0:T(1024)S(1)} fusion(bf16[768,768]{1,0:T(8,128)(2,1)} %get-tuple-element.216, bf16[12288,768]{1,0:T(8,128)(2,1)} %get-tuple-element.215, s32[]{:T(128)S(6)} %select_n.32, s32[768]{0:T(1024)S(1)} %get-tuple-element.214, s32[768]{0:T(1024)S(1)} %get-tuple-element.189, pred[768]{0:T(1024)(128)(4,1)S(1)} %get-tuple-element.190), kind=kOutput, calls=%fused_computation.4.clone.1 | convolution fusion | flops 908328192 | bytes 2369284 | tf_op jit(solution)/shard_map/while/body/eval_jaxpr/dot_general | solution.py:31
  178.1 2.8 %fusion.21 = f32[768]{0:T(1024)S(1)} fusion(bf16[768,768]{1,0:T(8,128)(2,1)} %get-tuple-element.216, bf16[12288,768]{1,0:T(8,128)(2,1)} %get-tuple-element.215, s32[]{:T(128)S(6)} %select_n.32, s32[768]{0:T(1024)S(1)} %get-tuple-element.214, s32[768]{0:T(1024)S(1)} %get-tuple-element.189, pred[768]{0:T(1024)(128)(4,1)S(1)} %get-tuple-element.190), kind=kOutput, calls=%fused_computation.4.clone.1 | convolution fusion | flops 908328192 | bytes 2369284 | tf_op jit(solution)/shard_map/while/body/eval_jaxpr/dot_general | solution.py:31
  181.0 2.8 %fusion.21 = f32[768]{0:T(1024)S(1)} fusion(bf16[768,768]{1,0:T(8,128)(2,1)} %get-tuple-element.216, bf16[12288,768]{1,0:T(8,128)(2,1)} %get-tuple-element.215, s32[]{:T(128)S(6)} %select_n.32, s32[768]{0:T(1024)S(1)} %get-tuple-element.214, s32[768]{0:T(1024)S(1)} %get-tuple-element.189, pred[768]{0:T(1024)(128)(4,1)S(1)} %get-tuple-element.190), kind=kOutput, calls=%fused_computation.4.clone.1 | convolution fusion | flops 908328192 | bytes 2369284 | tf_op jit(solution)/shard_map/while/body/eval_jaxpr/dot_general | solution.py:31
  184.0 2.8 %fusion.21 = f32[768]{0:T(1024)S(1)} fusion(bf16[768,768]{1,0:T(8,128)(2,1)} %get-tuple-element.216, bf16[12288,768]{1,0:T(8,128)(2,1)} %get-tuple-element.215, s32[]{:T(128)S(6)} %select_n.32, s32[768]{0:T(1024)S(1)} %get-tuple-element.214, s32[768]{0:T(1024)S(1)} %get-tuple-element.189, pred[768]{0:T(1024)(128)(4,1)S(1)} %get-tuple-element.190), kind=kOutput, calls=%fused_computation.4.clone.1 | convolution fusion | flops 908328192 | bytes 2369284 | tf_op jit(solution)/shard_map/while/body/eval_jaxpr/dot_general | solution.py:31
  186.9 2.8 %fusion.21 = f32[768]{0:T(1024)S(1)} fusion(bf16[768,768]{1,0:T(8,128)(2,1)} %get-tuple-element.216, bf16[12288,768]{1,0:T(8,128)(2,1)} %get-tuple-element.215, s32[]{:T(128)S(6)} %select_n.32, s32[768]{0:T(1024)S(1)} %get-tuple-element.214, s32[768]{0:T(1024)S(1)} %get-tuple-element.189, pred[768]{0:T(1024)(128)(4,1)S(1)} %get-tuple-element.190), kind=kOutput, calls=%fused_computation.4.clone.1 | convolution fusion | flops 908328192 | bytes 2369284 | tf_op jit(solution)/shard_map/while/body/eval_jaxpr/dot_general | solution.py:31
  189.9 2.8 %fusion.21 = f32[768]{0:T(1024)S(1)} fusion(bf16[768,768]{1,0:T(8,128)(2,1)} %get-tuple-element.216, bf16[12288,768]{1,0:T(8,128)(2,1)} %get-tuple-element.215, s32[]{:T(128)S(6)} %select_n.32, s32[768]{0:T(1024)S(1)} %get-tuple-element.214, s32[768]{0:T(1024)S(1)} %get-tuple-element.189, pred[768]{0:T(1024)(128)(4,1)S(1)} %get-tuple-element.190), kind=kOutput, calls=%fused_computation.4.clone.1 | convolution fusion | flops 908328192 | bytes 2369284 | tf_op jit(solution)/shard_map/while/body/eval_jaxpr/dot_general | solution.py:31
  193.4 7.3 %all-to-all-start.2 = ((f32[16,48,1]{1,2,0:T(1,128)}), f32[16,48,1]{1,2,0:T(1,128)S(1)}, u32[]{:S(2)}, u32[]{:S(2)}) async-start(f32[16,48,1]{1,2,0:T(1,128)} %bitcast.9), calls=%async_computation.2 | async-start | bytes 16384 | tf_op jit(solution)/shard_map/all_to_all | solution.py:51
  200.7 6.2 %all-to-all-done.2 = f32[16,48,1]{1,2,0:T(1,128)S(1)} async-done(((f32[16,48,1]{1,2,0:T(1,128)}), f32[16,48,1]{1,2,0:T(1,128)S(1)}, u32[]{:S(2)}, u32[]{:S(2)}) %all-to-all-start.2) | async-done | bytes 3104 | tf_op jit(solution)/shard_map/all_to_all | solution.py:51
  208.2 3.4 %gather_fusion = f32[512]{0:T(512)} fusion(f32[768]{0:T(1024)S(1)} %all_to_all.32, s32[1024]{0:T(1024)S(1)} %pad_clamp_fusion), kind=kCustom, calls=%fused_computation | custom fusion | bytes 6144 | tf_op jit(solution)/shard_map/gather | solution.py:52
  (49 shorter events, 5.6 us)
Async XLA Ops:
  6.5 139.0 %all-gather.3.cloned.1.call-start = ((), (), s32[]{:S(2)}) async-start(), calls=%async_computation.3 | async-start | bytes 20054016 | tf_op jit(solution)/shard_map/all_gather | solution.py:38
  42.6 11.3 %all-to-all-start = ((s32[16,48,1]{1,2,0:T(1,128)}), s32[16,48,1]{1,2,0:T(1,128)S(1)}, u32[]{:S(2)}, u32[]{:S(2)}) async-start(s32[16,48,1]{1,2,0:T(1,128)} %bitcast.5), calls=%async_computation | async-start | bytes 16384 | tf_op jit(solution)/shard_map/all_to_all | solution.py:25
  193.4 13.5 %all-to-all-start.2 = ((f32[16,48,1]{1,2,0:T(1,128)}), f32[16,48,1]{1,2,0:T(1,128)S(1)}, u32[]{:S(2)}, u32[]{:S(2)}) async-start(f32[16,48,1]{1,2,0:T(1,128)} %bitcast.9), calls=%async_computation.2 | async-start | bytes 16384 | tf_op jit(solution)/shard_map/all_to_all | solution.py:51
Sparse Core Ops, SparseCore 0:
  39.4 106.0 all-gather.2
where the time goes:
time: 220 us; the launch traced here: 218 us
  waiting for transfers between devices  81.9 us (37%)
  matrix products  45.2 us (21%)
  blocking collectives  45.1 us (20%)
  between operations  13.5 us (6%)
  starting transfers between devices  12.4 us (6%)
  other arithmetic  11 us (5%)
  local copies, waits for them, and re-layouts  8.85 us (4%)
    all_gather x1, waiting for transfers between devices, on_device(): lax.all_gather(recv_rows, 'grp', axis=0, tiled=True)  69.4 us
    dot_general x16, matrix products, fold_piece(): lax.dot_general(recv_rows, key_rows, (((1,), (1,)), ((), ())), preferred_...  45.2 us
    all_to_all x1, blocking collectives, on_device(): lax.all_to_all(send_rows, 'bulk', split_axis=0, concat_axis=0, tiled=True)  24.3 us
    all_gather x1, blocking collectives, on_device(): lax.all_gather(recv_order, 'grp', axis=0, tiled=True)  20.8 us
    all_to_all x1, starting transfers between devices, on_device(): lax.all_to_all(best, 'bulk', split_axis=0, concat_axis=0, tiled=True)  7.26 us
    all_to_all x1, waiting for transfers between devices, on_device(): lax.all_to_all(send_order, 'bulk', split_axis=0, concat_axis=0, tiled=True)  6.22 us
    all_to_all x1, waiting for transfers between devices, on_device(): lax.all_to_all(best, 'bulk', split_axis=0, concat_axis=0, tiled=True)  6.21 us
    all_to_all x1, starting transfers between devices, on_device(): lax.all_to_all(send_order, 'bulk', split_axis=0, concat_axis=0, tiled=True)  5.1 us
  transfers between devices with their start and end apart: 3, of which 3 were waited for; matrix products, arithmetic and copies ran while one was open for 2% of the time, Pallas kernels for 0%

commit v1 on v0

v1 whole, which is shorter than its diff:
```python
import functools

import jax
import jax.numpy as jnp
from jax import lax
from jax.experimental import pallas as pl
from jax.experimental.pallas import tpu as pltpu
from jax.sharding import PartitionSpec as P

CAP = 48
NX, NY, NZ = 4, 4, 8
N = 16
S = N * CAP
ROWS = 512
D = 768
BIG = 1e9
LAG = 1
F32 = jnp.float32
BF16 = jnp.bfloat16


def diag():
    return lax.broadcasted_iota(jnp.int32, (CAP, 128), 0) == lax.broadcasted_iota(jnp.int32, (CAP, 128), 1)


def to_rows(column):
    parts = column.reshape(N, CAP, 128)
    return jnp.max(jnp.where(diag()[None], parts, F32(-BIG)), axis=1)


def to_column(rows):
    parts = jnp.broadcast_to(rows[:, None, :], (N, CAP, 128))
    value = jnp.max(jnp.where(diag()[None], parts, F32(-BIG)), axis=2, keepdims=True)
    return jnp.broadcast_to(value, (N, CAP, 128)).reshape(S, 128)


def chunk(n):
    return pl.ds(pl.multiple_of(n * CAP, 16), CAP)


def kernel(emb, cluster, order, out,
           send, buf, slot, osend, orecv, oblk, ocol, olane, rowacc, colacc, res, rrecv, fsend, fin,
           local, d_send, d_recv, oc_send, oc_recv, ob_send, ob_recv, r_send, r_recv, f_send, f_recv):
    bulk, grp = lax.axis_index("bulk"), lax.axis_index("grp")
    x, y = bulk // NY, bulk % NY
    z, k = grp // 2, grp % 2
    sgn = 1 - 2 * k

    def dev(xx, yy, zz, kk):
        return (xx % NX) * NY + yy, zz * 2 + kk

    def remote(src, dst, s_sem, r_sem, target):
        return pltpu.make_async_remote_copy(
            src_ref=src, dst_ref=dst, send_sem=s_sem, recv_sem=r_sem,
            device_id=target, device_id_type=pl.DeviceIdType.MESH)

    x_one = dev(x + sgn + NX, y, z, k)
    mate_y = y + 1 - 2 * (y % 2)
    partner = dev(x, y, z, 1 - k)
    homes = [
        None,
        dev(x - sgn + NX, y, z, k),
        dev(x + 2, y, z, k),
        dev(x + 2 * k, mate_y, z, k),
        partner,
        dev(x + sgn + NX, y, z, 1 - k),
    ]
    users = [
        None,
        x_one,
        dev(x + 2, y, z, k),
        dev(x + 2 * k, mate_y, z, k),
        partner,
        dev(x + sgn + NX, y, z, 1 - k),
    ]
    users[5] = dev(x + sgn + NX, y, z, 1 - k)

    def route(n):
        i, half = n // 2, n % 2
        dz = (i % 2) * ((i + 1) // 2) + (1 - i % 2) * (NZ - i // 2)
        yy = half * (NY - 1 - y) + (1 - half) * y
        zz = (z + dz) % NZ
        return dev(x, yy, zz, k), (yy // 2) * NZ + zz, dev(x, yy, (z - dz + 2 * NZ) % NZ, k)

    barrier = pltpu.get_barrier_semaphore()

    def greet(n, carry):
        pl.semaphore_signal(barrier, inc=1, device_id=route(n)[0], device_id_type=pl.DeviceIdType.MESH)
        return carry

    lax.fori_loop(1, N, greet, 0)
    for target in (dev(x + 1, y, z, k), dev(x + 3, y, z, k), dev(x + 2, y, z, k), partner,
                   dev(x + 1, y, z, 1 - k), dev(x + 3, y, z, 1 - k), dev(x, mate_y, z, k), dev(x + 2, mate_y, z, k)):
        pl.semaphore_signal(barrier, inc=1, device_id=target, device_id_type=pl.DeviceIdType.MESH)

    values = emb[...].astype(F32)
    unit = (values * lax.rsqrt(jnp.sum(values * values, axis=1, keepdims=True) + 1e-06)).astype(BF16)
    lane = cluster[...]
    member = lax.broadcasted_iota(jnp.int32, (N, ROWS), 0) == lane
    upper = lax.broadcasted_iota(jnp.int32, (ROWS, ROWS), 0) < lax.broadcasted_iota(jnp.int32, (ROWS, ROWS), 1)
    before = lax.dot_general(
        member.astype(F32).astype(BF16), upper.astype(F32).astype(BF16), (((1,), (0,)), ((), ())),
        preferred_element_type=F32)
    rank = jnp.sum(jnp.where(member, before, F32(0.0)), axis=0, keepdims=True)
    slot[...] = jnp.broadcast_to(lane.astype(F32) * CAP + rank, (8, ROWS))
    orders = order[...].astype(F32)

    def place(begin, size):
        index = lax.broadcasted_iota(jnp.int32, (size, ROWS), 0).astype(F32) + F32(begin)
        return index == slot[0:1, :]

    ocols = []
    for t in range(4):
        hit = place(t * 192, 192)
        send[t * 192:(t + 1) * 192, :] = lax.dot_general(
            hit.astype(F32).astype(BF16), unit, (((1,), (0,)), ((), ())), preferred_element_type=F32).astype(BF16)
        ocols.append(jnp.broadcast_to(
            jnp.min(jnp.where(hit, orders, F32(BIG)), axis=1, keepdims=True), (192, 128)))
    osend[...] = jnp.broadcast_to(to_rows(jnp.concatenate(ocols, axis=0))[:, None, :], (N, 8, 128))
    rowacc[...] = jnp.full((6, S, 128), -1.0, F32)
    colacc[...] = jnp.full((6, 8, S), -1.0, F32)

    pl.semaphore_wait(barrier, N - 1 + 8)

    mine = (y // 2) * NZ + z
    own_rows = pltpu.make_async_copy(send.at[chunk(mine)], buf.at[0, chunk(0)], d_recv.at[0, 0])
    own_rows.start()
    own_order = pltpu.make_async_copy(osend.at[mine], orecv.at[0], local.at[0])
    own_order.start()

    def deal_orders(n, carry):
        target, c, _ = route(n)
        remote(osend.at[c], orecv.at[n], oc_send, oc_recv, target).start()
        return carry

    lax.fori_loop(1, N, deal_orders, 0)

    def deal_rows(n, carry):
        target, c, _ = route(n)
        remote(send.at[chunk(c)], buf.at[0, chunk(n)], d_send.at[0], d_recv.at[0, n], target).start()
        return carry

    lax.fori_loop(1, N, deal_rows, 0)

    def relay(source, n, block, target):
        return remote(buf.at[source, chunk(n)], buf.at[block, chunk(n)], d_send.at[block], d_recv.at[block, n], target)

    def arrived(block, n):
        pltpu.make_async_copy(buf.at[block, chunk(n)], buf.at[block, chunk(n)], d_recv.at[block, n]).wait()

    own_order.wait()
    all_but_one = pl.ds(1, N - 1)
    remote(osend.at[all_but_one], orecv.at[all_but_one], oc_send, oc_recv, partner).wait()
    oblk[0] = jnp.max(orecv[...], axis=1)

    def step(n, carry):
        @pl.when(n < N)
        def _():
            arrived(0, n)
            relay(0, n, 1, users[1]).start()
            relay(0, n, 4, users[4]).start()

        @pl.when(jnp.logical_and(n >= LAG, n < N + LAG))
        def _():
            m = n - LAG
            arrived(1, m)
            relay(1, m, 2, users[1]).start()
            relay(1, m, 5, users[4]).start()

        @pl.when(n >= 2 * LAG)
        def _():
            m = n - 2 * LAG
            arrived(2, m)
            relay(2 * k, m, 3, dev(x, mate_y, z, k)).start()

        return carry

    for b in range(1, 6):
        remote(oblk.at[0], oblk.at[b], ob_send.at[b], ob_recv.at[b], users[b]).start()
    lax.fori_loop(0, N + 2 * LAG, step, 0)
    for b in range(1, 6):
        remote(oblk.at[0], oblk.at[b], ob_send.at[b], ob_recv.at[b], users[b]).wait()

    def spread_orders(b, carry):
        column = to_column(oblk[b])
        ocol[b] = column
        olane[b] = jnp.transpose(column)[0:8, :]
        return carry

    lax.fori_loop(0, 6, spread_orders, 0)
    for b in range(3, 6):
        def drain(n, carry, b=b):
            arrived(b, n)
            return carry

        lax.fori_loop(0, N, drain, 0)

    def tile(i, j, c):
        cols = pl.ds(pl.multiple_of(c * 256, 256), 256)
        score = lax.dot_general(
            buf[i], buf[j, cols, :], (((1,), (1,)), ((), ())), preferred_element_type=F32)
        earlier = olane[j, 0:1, cols] < jnp.concatenate([ocol[i]] * 2, axis=1)
        return cols, score, earlier

    def self_tile(c, carry):
        _, score, earlier = tile(0, 0, c)
        seen = jnp.where(earlier, score, F32(-1.0))
        rowacc[0] = jnp.maximum(rowacc[0], jnp.maximum(seen[:, 0:128], seen[:, 128:256]))
        return carry

    lax.fori_loop(0, 3, self_tile, 0)

    def pair_tile(t, carry):
        u, c = t // 3, t % 3
        g1, g2 = (u + 5) // 7, u // 7
        i = 3 * (g1 - g2) + (2 + 2 * k) * g2
        j = (1 - g1) * (1 + u) + (g1 - g2) * (u - 3 + (u + 1) // 3) + g2 * (u - 3 - 4 * k)
        cols, score, earlier = tile(i, j, c)
        seen = jnp.where(earlier, score, F32(-1.0))
        rowacc[i] = jnp.maximum(rowacc[i], jnp.maximum(seen[:, 0:128], seen[:, 128:256]))
        other = jnp.where(earlier, F32(-1.0), score)
        colacc[j, :, cols] = jnp.maximum(colacc[j, :, cols], jnp.max(other.reshape(S // 8, 8, 256), axis=0))
        return carry

    lax.fori_loop(0, 27, pair_tile, 0)

    def collect(b, carry):
        column = jnp.max(rowacc[b], axis=1, keepdims=True)
        line = jnp.max(colacc[b], axis=0, keepdims=True)
        both = jnp.maximum(column, jnp.transpose(jnp.broadcast_to(line, (128, S))))
        res[b] = to_rows(both)
        return carry

    lax.fori_loop(0, 6, collect, 0)
    for b in range(1, 6):
        remote(res.at[b], rrecv.at[b], r_send.at[b], r_recv.at[b], homes[b]).start()
    rrecv[0] = res[0]
    for b in range(1, 6):
        remote(res.at[b], rrecv.at[b], r_send.at[b], r_recv.at[b], homes[b]).wait()
    best = jnp.max(rrecv[...], axis=0)
    fsend[...] = jnp.broadcast_to(best[:, None, :], (N, 8, 128))

    own_best = pltpu.make_async_copy(fsend.at[0], fin.at[mine], local.at[1])
    own_best.start()

    def give_back(n, carry):
        remote(fsend.at[n], fin.at[mine], f_send, f_recv, route(n)[2]).start()
        return carry

    lax.fori_loop(1, N, give_back, 0)
    remote(buf.at[0, pl.ds(0, S - CAP)], buf.at[0, pl.ds(0, S - CAP)], d_send.at[0], d_recv.at[0, 0], partner).wait_send()
    for b in range(1, 6):
        remote(buf.at[b], buf.at[b], d_send.at[b], d_recv.at[b, 0], partner).wait_send()
    own_best.wait()
    remote(fsend.at[all_but_one], fin.at[all_but_one], f_send, f_recv, partner).wait()
    column = to_column(jnp.max(fin[...], axis=1))
    total = jnp.full((8, ROWS), -BIG, F32)
    for t in range(4):
        hit = place(t * 192, 192)
        part = jnp.where(hit, jnp.concatenate([column[t * 192:(t + 1) * 192, :]] * 4, axis=1), F32(-BIG))
        total = jnp.maximum(total, jnp.max(part.reshape(24, 8, ROWS), axis=0))
    out[...] = jnp.max(total, axis=0, keepdims=True)


def on_device(embeddings, cluster_ids, row_order):
    vmem = pl.BlockSpec(memory_space=pltpu.VMEM)
    dma = pltpu.SemaphoreType.DMA
    result = pl.pallas_call(
        kernel,
        out_shape=jax.ShapeDtypeStruct((1, ROWS), F32),
        in_specs=[vmem] * 3,
        out_specs=vmem,
        scratch_shapes=[
            pltpu.VMEM((S, D), BF16),
            pltpu.VMEM((6, S, D), BF16),
            pltpu.VMEM((8, ROWS), F32),
            pltpu.VMEM((N, 8, 128), F32),
            pltpu.VMEM((N, 8, 128), F32),
            pltpu.VMEM((6, N, 128), F32),
            pltpu.VMEM((6, S, 128), F32),
            pltpu.VMEM((6, 8, S), F32),
            pltpu.VMEM((6, S, 128), F32),
            pltpu.VMEM((6, 8, S), F32),
            pltpu.VMEM((6, N, 128), F32),
            pltpu.VMEM((6, N, 128), F32),
            pltpu.VMEM((N, 8, 128), F32),
            pltpu.VMEM((N, 8, 128), F32),
            dma((2,)), dma((6,)), dma((6, N)), dma, dma, dma((6,)), dma((6,)), dma((6,)), dma((6,)), dma, dma,
        ],
        compiler_params=pltpu.CompilerParams(
            collective_id=0, has_side_effects=True, vmem_limit_bytes=60 * 1024 * 1024),
    )(embeddings, cluster_ids.reshape(1, ROWS), row_order.reshape(1, ROWS))
    return result.reshape(ROWS)


def solution(mesh):
    spec = P(("bulk", "grp"))
    return jax.shard_map(
        on_device,
        mesh=mesh,
        in_specs=(P(("bulk", "grp"), None), P(("bulk", "grp"), None), spec),
        out_specs=spec,
        check_vma=False,
    )
```

time: 220 us -> 94.5 us (0.43)
  Pallas kernels: 0 us -> 93.1 us
  waiting for transfers between devices: 81.9 us -> 0 us
  matrix products: 45.2 us -> 0 us
  blocking collectives: 45.1 us -> 0 us
  between operations: 13.5 us -> 0.01 us
  starting transfers between devices: 12.4 us -> 0 us
  other arithmetic: 11 us -> 0 us
  local copies, waits for them, and re-layouts: 8.85 us -> 1.26 us
    pallas_call x0 -> x1, Pallas kernels: none -> 93.1 us  [on_device(): pl.pallas_call(kernel, out_shape=jax.ShapeDtypeStruct((1, ROWS), F32), in...]
    all_gather x1 -> x0, waiting for transfers between devices: 69.4 us -> none  [on_device(): lax.all_gather(recv_rows, 'grp', axis=0, tiled=True)]
    dot_general x16 -> x0, matrix products: 45.2 us -> none  [fold_piece(): lax.dot_general(recv_rows, key_rows, (((1,), (1,)), ((), ())), preferred_...]
    all_to_all x1 -> x0, blocking collectives: 24.3 us -> none  [on_device(): lax.all_to_all(send_rows, 'bulk', split_axis=0, concat_axis=0, tiled=True)]
    all_gather x1 -> x0, blocking collectives: 20.8 us -> none  [on_device(): lax.all_gather(recv_order, 'grp', axis=0, tiled=True)]
    all_to_all x2 -> x0, waiting for transfers between devices: 12.4 us -> none  [the longest x1 6.22 us: on_device(): lax.all_to_all(send_order, 'bulk', split_axis=0, concat_axis=0, tiled=True)]
    all_to_all x2 -> x0, starting transfers between devices: 12.4 us -> none  [the longest x1 7.26 us: on_device(): lax.all_to_all(best, 'bulk', split_axis=0, concat_axis=0, tiled=True)]
    scatter x1 -> x0, other arithmetic: 3.52 us -> none  [on_device(): jnp.zeros((owners * capacity, width), jnp.bfloat16).at[slot].set(unit)]
  transfers between devices with their start and end apart: 3 -> 0, of which waited for: 3 -> 0; matrix products, arithmetic and copies ran while one was open for 2% -> 0% of each run, Pallas kernels for 0% -> 0%
where the time goes in v1:
time: 94.5 us; the launch traced here: 94.4 us
  Pallas kernels  93.1 us (99%)
  local copies, waits for them, and re-layouts  1.26 us (1%)
    pallas_call x1, Pallas kernels, on_device(): pl.pallas_call(kernel, out_shape=jax.ShapeDtypeStruct((1, ROWS), F32), in...  93.1 us

profile of v1, /device:TPU:8, one launch (start us, length us, event | category | flops | bytes accessed | tf_op | source)
XLA Modules:
  0.0 94.4 jit_solution(14454919844726995742)
XLA Ops:
  0.0 93.1 %shard_map.37 = f32[1,512]{1,0:T(1,128)} custom-call(bf16[512,768]{1,0:T(8,128)(2,1)} %emb.1, s32[1,512]{1,0:T(1,128)} %bitcast.4, s32[1,512]{1,0:T(1,128)} %bitcast.5), custom_call_target="tpu_custom_call" | custom-call | tf_op jit(solution)/shard_map/pallas_call | solution.py:268
  93.1 1.3 %copy.5 = f32[512]{0:T(512)} copy(f32[512]{0:T(512)} %bitcast.3) | data formatting | bytes 4096

commit v2 on v1

--- a/solution.py
+++ b/solution.py
@@ -14,7 +14,7 @@
 ROWS = 512
 D = 768
 BIG = 1e9
-LAG = 1
+LAG = 2
 F32 = jnp.float32
 BF16 = jnp.bfloat16
 
@@ -40,7 +40,7 @@
 
 def kernel(emb, cluster, order, out,
            send, buf, slot, osend, orecv, oblk, ocol, olane, rowacc, colacc, res, rrecv, fsend, fin,
-           local, d_send, d_recv, oc_send, oc_recv, ob_send, ob_recv, r_send, r_recv, f_send, f_recv):
+           mid, local, m_send, m_recv, d_send, d_recv, oc_send, oc_recv, ob_send, ob_recv, r_send, r_recv, f_send, f_recv):
     bulk, grp = lax.axis_index("bulk"), lax.axis_index("grp")
     x, y = bulk // NY, bulk % NY
     z, k = grp // 2, grp % 2
@@ -73,7 +73,6 @@
         partner,
         dev(x + sgn + NX, y, z, 1 - k),
     ]
-    users[5] = dev(x + sgn + NX, y, z, 1 - k)
 
     def route(n):
         i, half = n // 2, n % 2
@@ -118,7 +117,7 @@
             jnp.min(jnp.where(hit, orders, F32(BIG)), axis=1, keepdims=True), (192, 128)))
     osend[...] = jnp.broadcast_to(to_rows(jnp.concatenate(ocols, axis=0))[:, None, :], (N, 8, 128))
     rowacc[...] = jnp.full((6, S, 128), -1.0, F32)
-    colacc[...] = jnp.full((6, 8, S), -1.0, F32)
+    colacc[...] = jnp.full((7, 8, S), -1.0, F32)
 
     pl.semaphore_wait(barrier, N - 1 + 8)
 
@@ -128,19 +127,40 @@
     own_order = pltpu.make_async_copy(osend.at[mine], orecv.at[0], local.at[0])
     own_order.start()
 
-    def deal_orders(n, carry):
+    def deal(n):
+        target, c, _ = route(n)
+        remote(send.at[chunk(c)], buf.at[0, chunk(n)], d_send.at[0], d_recv.at[0, n], target).start()
+
+    def deal_order(n):
         target, c, _ = route(n)
         remote(osend.at[c], orecv.at[n], oc_send, oc_recv, target).start()
-        return carry
-
-    lax.fori_loop(1, N, deal_orders, 0)
-
-    def deal_rows(n, carry):
+
+    via = dev(x, y, (z + NZ - 2) % NZ, k)
+
+    def deal_far(n):
         target, c, _ = route(n)
-        remote(send.at[chunk(c)], buf.at[0, chunk(n)], d_send.at[0], d_recv.at[0, n], target).start()
-        return carry
-
-    lax.fori_loop(1, N, deal_rows, 0)
+
+        @pl.when(k == 0)
+        def _():
+            remote(send.at[chunk(c)], buf.at[0, chunk(n)], d_send.at[0], d_recv.at[0, n], target).start()
+
+        @pl.when(k == 1)
+        def _():
+            remote(send.at[chunk(c)], mid.at[chunk(n - 14)], d_send.at[0], m_recv.at[n - 14], via).start()
+
+    def pass_on(n):
+        yy = (n % 2) * (NY - 1 - y) + (1 - n % 2) * y
+        pltpu.make_async_copy(mid.at[chunk(n - 14)], mid.at[chunk(n - 14)], m_recv.at[n - 14]).wait()
+        remote(mid.at[chunk(n - 14)], buf.at[0, chunk(n)], m_send, d_recv.at[0, n],
+               dev(x, yy, (z + NZ - 2) % NZ, k)).start()
+
+    for n in range(1, N):
+        deal_order(n)
+    for n in (1, 2, 3, 4, 5, 6, 7, 8, 9, 14, 15, 10, 11, 12, 13):
+        if n < 14:
+            deal(n)
+        else:
+            deal_far(n)
 
     def relay(source, n, block, target):
         return remote(buf.at[source, chunk(n)], buf.at[block, chunk(n)], d_send.at[block], d_recv.at[block, n], target)
@@ -148,10 +168,63 @@
     def arrived(block, n):
         pltpu.make_async_copy(buf.at[block, chunk(n)], buf.at[block, chunk(n)], d_recv.at[block, n]).wait()
 
-    own_order.wait()
     all_but_one = pl.ds(1, N - 1)
-    remote(osend.at[all_but_one], orecv.at[all_but_one], oc_send, oc_recv, partner).wait()
-    oblk[0] = jnp.max(orecv[...], axis=1)
+
+    def share_orders():
+        own_order.wait()
+        remote(osend.at[all_but_one], orecv.at[all_but_one], oc_send, oc_recv, partner).wait()
+        oblk[0] = jnp.max(orecv[...], axis=1)
+        for b in range(1, 6):
+            remote(oblk.at[0], oblk.at[b], ob_send.at[b], ob_recv.at[b], users[b]).start()
+
+    def spread_orders(b, carry):
+        column = to_column(oblk[b])
+        ocol[b] = column
+        olane[b] = jnp.transpose(column)[0:8, :]
+        return carry
+
+    def take_orders():
+        for b in range(1, 6):
+            remote(oblk.at[0], oblk.at[b], ob_send.at[b], ob_recv.at[b], users[b]).wait()
+        lax.fori_loop(0, 6, spread_orders, 0)
+
+    def drain(begin, end):
+        for b in range(3, 6):
+            def one(n, carry, b=b):
+                arrived(b, n)
+                return carry
+
+            lax.fori_loop(begin, end, one, 0)
+
+    def pair(v):
+        u = v - 1
+        real = (v + 9) // 10
+        g1, g2 = (u + 5) // 7, u // 7
+        i = (3 * (g1 - g2) + (2 + 2 * k) * g2) * real
+        j = ((1 - g1) * (1 + u) + (g1 - g2) * (u - 3 + (u + 1) // 3) + g2 * (u - 3 - 4 * k)) * real
+        return i, j, j + 6 * (1 - real)
+
+    def compare(i, j, to, begin, size, c):
+        rows = pl.ds(begin, size)
+        cols = pl.ds(pl.multiple_of(c * 256, 256), 256)
+        score = lax.dot_general(
+            buf[i, rows, :], buf[j, cols, :], (((1,), (1,)), ((), ())), preferred_element_type=F32)
+        earlier = olane[j, 0:1, cols] < jnp.concatenate([ocol[i, rows, :]] * 2, axis=1)
+        seen = jnp.where(earlier, score, F32(-1.0))
+        rowacc[i, rows, :] = jnp.maximum(rowacc[i, rows, :], jnp.maximum(seen[:, 0:128], seen[:, 128:256]))
+        other = jnp.where(earlier, F32(-1.0), score)
+        colacc[to, :, cols] = jnp.maximum(
+            colacc[to, :, cols], jnp.max(other.reshape(size // 8, 8, 256), axis=0))
+
+    def tile(v, r, c):
+        i, j, to = pair(v)
+        compare(i, j, to, pl.multiple_of(r * 256, 256), 256, c)
+
+    def first(v, carry):
+        tile(v, 0, 0)
+        return carry
+
+    gap = 2 * LAG
 
     def step(n, carry):
         @pl.when(n < N)
@@ -167,62 +240,72 @@
             relay(1, m, 2, users[1]).start()
             relay(1, m, 5, users[4]).start()
 
-        @pl.when(n >= 2 * LAG)
-        def _():
-            m = n - 2 * LAG
+        @pl.when(jnp.logical_and(n >= gap, n < N + gap))
+        def _():
+            m = n - gap
             arrived(2, m)
             relay(2 * k, m, 3, dev(x, mate_y, z, k)).start()
 
-        return carry
-
-    for b in range(1, 6):
-        remote(oblk.at[0], oblk.at[b], ob_send.at[b], ob_recv.at[b], users[b]).start()
-    lax.fori_loop(0, N + 2 * LAG, step, 0)
-    for b in range(1, 6):
-        remote(oblk.at[0], oblk.at[b], ob_send.at[b], ob_recv.at[b], users[b]).wait()
-
-    def spread_orders(b, carry):
-        column = to_column(oblk[b])
-        ocol[b] = column
-        olane[b] = jnp.transpose(column)[0:8, :]
-        return carry
-
-    lax.fori_loop(0, 6, spread_orders, 0)
-    for b in range(3, 6):
-        def drain(n, carry, b=b):
-            arrived(b, n)
-            return carry
-
-        lax.fori_loop(0, N, drain, 0)
-
-    def tile(i, j, c):
-        cols = pl.ds(pl.multiple_of(c * 256, 256), 256)
-        score = lax.dot_general(
-            buf[i], buf[j, cols, :], (((1,), (1,)), ((), ())), preferred_element_type=F32)
-        earlier = olane[j, 0:1, cols] < jnp.concatenate([ocol[i]] * 2, axis=1)
-        return cols, score, earlier
-
-    def self_tile(c, carry):
-        _, score, earlier = tile(0, 0, c)
-        seen = jnp.where(earlier, score, F32(-1.0))
-        rowacc[0] = jnp.maximum(rowacc[0], jnp.maximum(seen[:, 0:128], seen[:, 128:256]))
-        return carry
-
-    lax.fori_loop(0, 3, self_tile, 0)
-
-    def pair_tile(t, carry):
-        u, c = t // 3, t % 3
-        g1, g2 = (u + 5) // 7, u // 7
-        i = 3 * (g1 - g2) + (2 + 2 * k) * g2
-        j = (1 - g1) * (1 + u) + (g1 - g2) * (u - 3 + (u + 1) // 3) + g2 * (u - 3 - 4 * k)
-        cols, score, earlier = tile(i, j, c)
-        seen = jnp.where(earlier, score, F32(-1.0))
-        rowacc[i] = jnp.maximum(rowacc[i], jnp.maximum(seen[:, 0:128], seen[:, 128:256]))
-        other = jnp.where(earlier, F32(-1.0), score)
-        colacc[j, :, cols] = jnp.maximum(colacc[j, :, cols], jnp.max(other.reshape(S // 8, 8, 256), axis=0))
-        return carry
-
-    lax.fori_loop(0, 27, pair_tile, 0)
+        @pl.when(n == 6)
+        def _():
+            share_orders()
+
+        @pl.when(jnp.logical_and(n == 8, k == 1))
+        def _():
+            pass_on(14)
+            pass_on(15)
+
+        @pl.when(n == 10)
+        def _():
+            take_orders()
+
+        @pl.when(n == 11)
+        def _():
+            drain(0, 6)
+
+        @pl.when(jnp.logical_and(n >= 11, n < 14))
+        def _():
+            lax.fori_loop((n - 11) * 3, (n - 11) * 3 + 3 + n // 13, first, 0)
+
+        @pl.when(n == 17)
+        def _():
+            drain(6, 11)
+
+        @pl.when(n >= 14)
+        def _():
+            def second(q, carry):
+                tile(n - 14, 1 - q % 2, (q + 1) // 2)
+                return carry
+
+            lax.fori_loop(0, 3, second, 0)
+
+        return carry
+
+    lax.fori_loop(0, 24, step, 0)
+    drain(11, N)
+
+    side_x, side_y = 1 - x // 2, 1 - y % 2
+
+    def third(v, carry):
+        i, j, to = pair(v)
+        shared = jnp.logical_or(jnp.logical_or(v == 2, v == 3), v == 5)
+        lead = jnp.where(v == 2, side_x, jnp.where(v == 3, side_y, 1 - side_y))
+
+        @pl.when(jnp.logical_or(jnp.logical_not(shared), lead == 1))
+        def _():
+            compare(i, j, to, 0, 768, 2)
+
+        @pl.when(jnp.logical_not(shared))
+        def _():
+            compare(j, i, i, 0, 512, 2)
+
+        @pl.when(jnp.logical_and(shared, lead == 0))
+        def _():
+            compare(i, j, j, 0, 512, 2)
+
+        return carry
+
+    lax.fori_loop(0, 10, third, 0)
 
     def collect(b, carry):
         column = jnp.max(rowacc[b], axis=1, keepdims=True)
@@ -251,6 +334,10 @@
     remote(buf.at[0, pl.ds(0, S - CAP)], buf.at[0, pl.ds(0, S - CAP)], d_send.at[0], d_recv.at[0, 0], partner).wait_send()
     for b in range(1, 6):
         remote(buf.at[b], buf.at[b], d_send.at[b], d_recv.at[b, 0], partner).wait_send()
+    @pl.when(k == 1)
+    def _():
+        pltpu.make_async_copy(mid, mid, m_send).wait()
+
     own_best.wait()
     remote(fsend.at[all_but_one], fin.at[all_but_one], f_send, f_recv, partner).wait()
     column = to_column(jnp.max(fin[...], axis=1))
@@ -280,12 +367,13 @@
             pltpu.VMEM((6, S, 128), F32),
             pltpu.VMEM((6, 8, S), F32),
             pltpu.VMEM((6, S, 128), F32),
-            pltpu.VMEM((6, 8, S), F32),
+            pltpu.VMEM((7, 8, S), F32),
             pltpu.VMEM((6, N, 128), F32),
             pltpu.VMEM((6, N, 128), F32),
             pltpu.VMEM((N, 8, 128), F32),
             pltpu.VMEM((N, 8, 128), F32),
-            dma((2,)), dma((6,)), dma((6, N)), dma, dma, dma((6,)), dma((6,)), dma((6,)), dma((6,)), dma, dma,
+            pltpu.VMEM((2 * CAP, D), BF16),
+            dma((2,)), dma, dma((2,)), dma((6,)), dma((6, N)), dma, dma, dma((6,)), dma((6,)), dma((6,)), dma((6,)), dma, dma,
         ],
         compiler_params=pltpu.CompilerParams(
             collective_id=0, has_side_effects=True, vmem_limit_bytes=60 * 1024 * 1024),

time: 94.5 us -> 82.3 us (0.87); the launches traced: 94.4 us -> 80.6 us
  Pallas kernels: 93.1 us -> 79.4 us
    pallas_call x1, Pallas kernels: 93.1 us -> 79.4 us  [on_device(): pl.pallas_call(kernel, out_shape=jax.ShapeDtypeStruct((1, ROWS), F32), in...]
where the time goes in v2:
time: 82.3 us; the launch traced here: 80.6 us
  Pallas kernels  79.4 us (96%)
  local copies, waits for them, and re-layouts  1.26 us (2%)
    pallas_call x1, Pallas kernels, on_device(): pl.pallas_call(kernel, out_shape=jax.ShapeDtypeStruct((1, ROWS), F32), in...  79.4 us

profile of v2, /device:TPU:8, one launch (start us, length us, event | category | flops | bytes accessed | tf_op | source)
XLA Modules:
  0.0 80.6 jit_solution(18143251050415935550)
XLA Ops:
  0.0 79.4 %shard_map.37 = f32[1,512]{1,0:T(1,128)} custom-call(bf16[512,768]{1,0:T(8,128)(2,1)} %emb.1, s32[1,512]{1,0:T(1,128)} %bitcast.4, s32[1,512]{1,0:T(1,128)} %bitcast.5), custom_call_target="tpu_custom_call" | custom-call | tf_op jit(solution)/shard_map/pallas_call | solution.py:355
  79.4 1.3 %copy.5 = f32[512]{0:T(512)} copy(f32[512]{0:T(512)} %bitcast.3) | data formatting | bytes 4096

commit v3 on v2

--- a/solution.py
+++ b/solution.py
@@ -224,6 +224,12 @@
         tile(v, 0, 0)
         return carry
 
+    def second(v, carry):
+        i, j, to = pair(v)
+        compare(i, j, to, 0, 512, 1)
+        compare(j, i, i, 0, 256, 1)
+        return carry
+
     gap = 2 * LAG
 
     def step(n, carry):
@@ -267,21 +273,18 @@
         def _():
             lax.fori_loop((n - 11) * 3, (n - 11) * 3 + 3 + n // 13, first, 0)
 
-        @pl.when(n == 17)
+        @pl.when(n == 16)
         def _():
             drain(6, 11)
 
         @pl.when(n >= 14)
         def _():
-            def second(q, carry):
-                tile(n - 14, 1 - q % 2, (q + 1) // 2)
-                return carry
-
-            lax.fori_loop(0, 3, second, 0)
-
-        return carry
-
-    lax.fori_loop(0, 24, step, 0)
+            m = n - 14
+            lax.fori_loop(2 * m - jnp.minimum(m, 1), jnp.minimum(2 * m + 1, 10), second, 0)
+
+        return carry
+
+    lax.fori_loop(0, N + gap, step, 0)
     drain(11, N)
 
     side_x, side_y = 1 - x // 2, 1 - y % 2
@@ -305,7 +308,10 @@
 
         return carry
 
-    lax.fori_loop(0, 10, third, 0)
+    def most(t, carry):
+        return third(t + 3 - (t // 7) * (2 * t - 6), carry)
+
+    lax.fori_loop(0, 9, most, 0)
 
     def collect(b, carry):
         column = jnp.max(rowacc[b], axis=1, keepdims=True)
@@ -314,9 +320,11 @@
         res[b] = to_rows(both)
         return carry
 
-    lax.fori_loop(0, 6, collect, 0)
+    lax.fori_loop(1, 6, collect, 0)
     for b in range(1, 6):
         remote(res.at[b], rrecv.at[b], r_send.at[b], r_recv.at[b], homes[b]).start()
+    third(0, 0)
+    collect(0, 0)
     rrecv[0] = res[0]
     for b in range(1, 6):
         remote(res.at[b], rrecv.at[b], r_send.at[b], r_recv.at[b], homes[b]).wait()

time: 82.3 us -> 78.8 us (0.957); the launches traced: 80.6 us -> 78.7 us
  Pallas kernels: 79.4 us -> 77.5 us
    pallas_call x1, Pallas kernels: 79.4 us -> 77.5 us  [on_device(): pl.pallas_call(kernel, out_shape=jax.ShapeDtypeStruct((1, ROWS), F32), in...]
where the time goes in v3:
time: 78.8 us; the launch traced here: 78.7 us
  Pallas kernels  77.5 us (98%)
  local copies, waits for them, and re-layouts  1.26 us (2%)
    pallas_call x1, Pallas kernels, on_device(): pl.pallas_call(kernel, out_shape=jax.ShapeDtypeStruct((1, ROWS), F32), in...  77.5 us

profile of v3, /device:TPU:8, one launch (start us, length us, event | category | flops | bytes accessed | tf_op | source)
XLA Modules:
  0.0 78.7 jit_solution(354656257928933864)
XLA Ops:
  0.0 77.5 %shard_map.37 = f32[1,512]{1,0:T(1,128)} custom-call(bf16[512,768]{1,0:T(8,128)(2,1)} %emb.1, s32[1,512]{1,0:T(1,128)} %bitcast.4, s32[1,512]{1,0:T(1,128)} %bitcast.5), custom_call_target="tpu_custom_call" | custom-call | tf_op jit(solution)/shard_map/pallas_call | solution.py:363
  77.5 1.3 %copy.5 = f32[512]{0:T(512)} copy(f32[512]{0:T(512)} %bitcast.3) | data formatting | bytes 4096
